TPU v7x, 512 devices: a whole 4x8x8 slice. The times are simulated.
512 devices in a mesh: dp: 16 (over z, core), tp: 4 (over y_lo), cp: 8 (over y_hi, x).
Axes of the slice: x: 4, y: 8 (y_hi: 2, y_lo: 4; y = y_hi * 4 + y_lo), z: 8, core: 2. Of those that a mesh axis runs over, the one named last changes fastest.
Arguments:
- tokens: bfloat16 [65536, 1024], P(('dp', 'tp', 'cp')), may hold values from -6 to 6
- expert_ids: int32 [65536, 2], P(('dp', 'tp', 'cp')), may hold values from 0 to 31, all different within a row; in each aligned block of 128 rows (0 to 127, 128 to 255, ...) at most 12 rows name the same one
- router_weight: bfloat16 [1024, 32], replicated, may hold values from -0.1875 to 0.1875
- gate_weight: bfloat16 [32, 1024, 384], P(('tp', 'cp'), 'dp'), may hold values from -0.1875 to 0.1875
- up_weight: bfloat16 [32, 1024, 384], P(('tp', 'cp'), 'dp'), may hold values from -0.1875 to 0.1875
- down_weight: bfloat16 [32, 384, 1024], P(('tp', 'cp'), None, 'dp'), may hold values from -0.3125 to 0.3125
- grad_out: bfloat16 [65536, 1024], P(('dp', 'tp', 'cp')), may hold values from -6 to 6
Outputs:
- moe_out: bfloat16 [65536, 1024], P(('dp', 'tp', 'cp'))
- grad_tokens: bfloat16 [65536, 1024], P(('dp', 'tp', 'cp'))
- router_grad: float32 [1024, 32], replicated
Inputs may be any that keep to these rules, and one draw needn't show every extreme that they name: `expert_ids`: each row names 2 different experts. Among the 128 rows of one device no expert is named by more than 12 rows, a bound that some block reaches.
All inputs are finite; a program needn't handle non-finite values.
Results may differ from a plain program's by a relative error of at most 0.0064.
Values may be sent and summed in bfloat16 or wider, within the bound.
A program may use at most 64 MiB of HBM per device.

v0:
```python
import jax
import jax.numpy as jnp
from jax import lax
from jax.sharding import PartitionSpec as P


def route_slots(flat_ids, expert_count):
    hits = (flat_ids[:, None] == jnp.arange(expert_count, dtype=jnp.int32)[None, :]).astype(
        jnp.int32
    )
    before = jnp.cumsum(hits, axis=0) - hits
    return jnp.sum(before * hits, axis=1)


def trade(stacked, capacity):
    item_count = stacked.shape[0]
    feature_dim = stacked.shape[2]
    tp_count = lax.axis_size("tp")
    cp_count = lax.axis_size("cp")
    shaped = stacked.reshape(item_count, tp_count * cp_count, capacity, feature_dim)
    moved = lax.all_to_all(shaped, ("tp", "cp"), split_axis=1, concat_axis=1, tiled=True)
    return moved.reshape(item_count, -1, feature_dim)


def expert_forward(received, w_gate, w_up, w_down):
    gate_act = jnp.dot(received, w_gate, preferred_element_type=jnp.float32)
    up_act = jnp.dot(received, w_up, preferred_element_type=jnp.float32)
    hidden = (jax.nn.silu(gate_act) * up_act).astype(jnp.bfloat16)
    produced = jnp.dot(hidden, w_down, preferred_element_type=jnp.float32).astype(jnp.bfloat16)
    return (gate_act, up_act, produced)


def expert_backward(received_grad, gate_act, up_act, w_gate, w_up, w_down):
    contract = (((1,), (1,)), ((), ()))
    grad_hidden = lax.dot_general(
        received_grad, w_down, contract, preferred_element_type=jnp.float32
    )
    sigma = jax.nn.sigmoid(gate_act)
    grad_gate = (grad_hidden * up_act * sigma * (1.0 + gate_act * (1.0 - sigma))).astype(
        jnp.bfloat16
    )
    grad_up = (grad_hidden * gate_act * sigma).astype(jnp.bfloat16)
    returned = lax.dot_general(grad_gate, w_gate, contract, preferred_element_type=jnp.float32)
    returned = returned + lax.dot_general(
        grad_up, w_up, contract, preferred_element_type=jnp.float32
    )
    return returned.astype(jnp.bfloat16)


def on_device(tokens, expert_ids, router_weight, gate_weight, up_weight, down_weight, grad_out):
    row_count, feature_dim = tokens.shape
    topk = expert_ids.shape[1]
    groups = lax.axis_size(("tp", "cp"))
    capacity = 3 * row_count * topk // (2 * groups)
    expert_count = router_weight.shape[1]
    contract = (((1,), (1,)), ((), ()))
    w_gate, w_up, w_down = (
        lax.all_gather(gate_weight[0], "dp", axis=0, tiled=True),
        lax.all_gather(up_weight[0], "dp", axis=0, tiled=True),
        lax.all_gather(down_weight[0], "dp", axis=1, tiled=True),
    )
    logits = jnp.dot(tokens, router_weight, preferred_element_type=jnp.float32)
    chosen = jnp.take_along_axis(logits, expert_ids, axis=1)
    mixing = 1.0 / jnp.sum(jnp.exp(chosen[:, None, :] - chosen[:, :, None]), axis=2)
    flat_ids = expert_ids.reshape(-1)
    slots = route_slots(flat_ids, expert_count)
    position = flat_ids * capacity + slots
    slot_total = groups * capacity
    repeated = jnp.repeat(tokens, topk, axis=0)
    scaled_grad = (mixing[:, :, None] * grad_out.astype(jnp.float32)[:, None, :]).astype(
        jnp.bfloat16
    )
    scaled_flat = scaled_grad.reshape(-1, feature_dim)
    sent = jnp.zeros((1, slot_total, feature_dim), jnp.bfloat16).at[0, position].set(repeated)
    received = trade(sent, capacity)[0]
    gate_act, up_act, produced = expert_forward(received, w_gate, w_up, w_down)
    came_back = trade(produced[None], capacity)[0]
    sent_grad = (
        jnp.zeros((1, slot_total, feature_dim), jnp.bfloat16).at[0, position].set(scaled_flat)
    )
    received_grad = trade(sent_grad, capacity)[0]
    returned = expert_backward(received_grad, gate_act, up_act, w_gate, w_up, w_down)
    back_home = trade(returned[None], capacity)[0]
    out_rows = jnp.take(came_back, position, axis=0).reshape(row_count, topk, feature_dim)
    moe_out = jnp.sum(mixing[:, :, None] * out_rows.astype(jnp.float32), axis=1).astype(
        jnp.bfloat16
    )
    back_rows = jnp.take(back_home, position, axis=0).reshape(row_count, topk, feature_dim)
    scores = jnp.einsum("td,tkd->tk", grad_out, out_rows, preferred_element_type=jnp.float32)
    dlogit = mixing * (scores - jnp.sum(mixing * scores, axis=1, keepdims=True))
    onehot = (
        expert_ids[:, :, None] == jnp.arange(expert_count, dtype=jnp.int32)[None, None, :]
    ).astype(jnp.float32)
    dense = jnp.sum(onehot * dlogit[:, :, None], axis=1).astype(jnp.bfloat16)
    router_back = lax.dot_general(
        dense, router_weight, contract, preferred_element_type=jnp.float32
    )
    grad_tokens = (jnp.sum(back_rows.astype(jnp.float32), axis=1) + router_back).astype(
        jnp.bfloat16
    )
    router_part = lax.dot_general(
        tokens, dense, (((0,), (0,)), ((), ())), preferred_element_type=jnp.float32
    )
    router_grad = lax.psum(router_part, ("dp", "tp", "cp"))
    return (moe_out, grad_tokens, router_grad)


def solution(mesh):
    in_specs = (
        P(("dp", "tp", "cp"), None),
        P(("dp", "tp", "cp"), None),
        P(),
        P(("tp", "cp"), "dp", None),
        P(("tp", "cp"), "dp", None),
        P(("tp", "cp"), None, "dp"),
        P(("dp", "tp", "cp"), None),
    )
    out_specs = (P(("dp", "tp", "cp"), None), P(("dp", "tp", "cp"), None), P())
    return jax.shard_map(
        on_device, mesh=mesh, in_specs=in_specs, out_specs=out_specs, check_vma=False
    )
```

profile of v0, /device:TPU:1, one launch (start us, length us, event | category | flops | bytes accessed | tf_op | source)
XLA Modules:
  0.0 453.8 jit_solution(12045069232960749352)
XLA Ops:
  10.1 1.2 broadcast_in_dim.16
  11.6 1.9 scatter_custom_fusion
  13.5 1.2 reshape.105
  14.7 10.6 %all-to-all-start = ((bf16[1,32,12,1024]{3,2,0,1:T(8,128)(2,1)}), bf16[1,32,12,1024]{3,2,0,1:T(8,128)(2,1)S(1)}, u32[]{:S(2)}, u32[]{:S(2)}) async-start(bf16[1,32,12,1024]{3,2,0,1:T(8,128)(2,1)} %bitcast.4), calls=%async_computation | async-start | bytes 2097152 | tf_op jit(solution)/shard_map/all_to_all | solution.py:21
  25.3 27.5 %all-gather.2 = bf16[1,384,1024]{1,2,0:T(8,128)(2,1)} all-gather(bf16[1,384,64]{1,2,0:T(8,128)(2,1)S(1)} %copy-done.15), channel_id=4, replica_groups=mesh['dp'=16,'tp'=4,'cp'=8] {'dp'}, dimensions={2}, use_global_device_ids=true | all-gather | bytes 835584 | tf_op jit(solution)/shard_map/all_gather | solution.py:60
  52.9 16.6 %all-gather.1 = bf16[1,1024,384]{2,1,0:T(8,128)(2,1)S(1)} all-gather(bf16[1,64,384]{2,1,0:T(8,128)(2,1)S(1)} %copy-done.16), channel_id=3, replica_groups=mesh['dp'=16,'tp'=4,'cp'=8] {'dp'}, dimensions={1}, use_global_device_ids=true | all-gather | bytes 835584 | tf_op jit(solution)/shard_map/all_gather | solution.py:59
  69.5 17.9 %all-gather = bf16[1,1024,384]{2,1,0:T(8,128)(2,1)S(1)} all-gather(bf16[1,64,384]{2,1,0:T(8,128)(2,1)S(1)} %copy-done.17), channel_id=2, replica_groups=mesh['dp'=16,'tp'=4,'cp'=8] {'dp'}, dimensions={1}, use_global_device_ids=true | all-gather | bytes 835584 | tf_op jit(solution)/shard_map/all_gather | solution.py:58
  90.5 1.2 reshape_broadcast_in_dim.6
  91.8 9.6 %all-to-all-start.1 = ((bf16[1,32,12,1024]{3,2,0,1:T(8,128)(2,1)}), bf16[1,32,12,1024]{3,2,0,1:T(8,128)(2,1)S(1)}, u32[]{:S(2)}, u32[]{:S(2)}) async-start(bf16[1,32,12,1024]{3,2,0,1:T(8,128)(2,1)} %bitcast.8), calls=%async_computation.1 | async-start | bytes 2097152 | tf_op jit(solution)/shard_map/all_to_all | solution.py:21
  101.9 2.0 gather_fusion
  104.4 1.7 mul.98
  106.1 21.9 %all-to-all-done.1 = bf16[1,32,12,1024]{3,2,0,1:T(8,128)(2,1)S(1)} async-done(((bf16[1,32,12,1024]{3,2,0,1:T(8,128)(2,1)}), bf16[1,32,12,1024]{3,2,0,1:T(8,128)(2,1)S(1)}, u32[]{:S(2)}, u32[]{:S(2)}) %all-to-all-start.1) | async-done | bytes 786464 | tf_op jit(solution)/shard_map/all_to_all | solution.py:21
  128.3 1.2 gather_fusion.1
  131.3 2.0 scatter_custom_fusion.1
  133.5 33.6 %all_to_all.20 = bf16[1,32,12,1024]{3,2,0,1:T(8,128)(2,1)S(1)} all-to-all(bf16[1,32,12,1024]{3,2,0,1:T(8,128)(2,1)S(1)} %bitcast.72), channel_id=1, replica_groups=mesh['dp'=16,'tp'=4,'cp'=8] {'tp','cp'}, dimensions={1} | all-to-all | bytes 1572864 | tf_op jit(solution)/shard_map/all_to_all | solution.py:21
  167.3 1.8 fusion.1
  170.9 1.2 reshape_broadcast_in_dim.7
  172.1 6.0 %all-to-all-start.3 = ((bf16[1,32,12,1024]{3,2,0,1:T(8,128)(2,1)}), bf16[1,32,12,1024]{3,2,0,1:T(8,128)(2,1)S(1)}, u32[]{:S(2)}, u32[]{:S(2)}) async-start(bf16[1,32,12,1024]{3,2,0,1:T(8,128)(2,1)} %bitcast.10), calls=%async_computation.3 | async-start | bytes 2097152 | tf_op jit(solution)/shard_map/all_to_all | solution.py:21
  179.0 2.1 multiply_reduce_fusion
  181.2 22.9 %all-to-all-done.3 = bf16[1,32,12,1024]{3,2,0,1:T(8,128)(2,1)S(1)} async-done(((bf16[1,32,12,1024]{3,2,0,1:T(8,128)(2,1)}), bf16[1,32,12,1024]{3,2,0,1:T(8,128)(2,1)S(1)}, u32[]{:S(2)}, u32[]{:S(2)}) %all-to-all-start.3) | async-done | bytes 786464 | tf_op jit(solution)/shard_map/all_to_all | solution.py:21
  204.2 1.2 gather_fusion.2
  206.1 1.2 reduce_sum.60
  208.3 237.0 %all-reduce.3.cloned.1.call-done = f32[1024,32]{0,1:T(8,128)} async-done(((f32[1024,32]{0,1:T(8,128)}), f32[1024,32]{0,1:T(8,128)}) %all-reduce.3.cloned.1.call-update) | async-done | bytes 131088 | tf_op jit(solution)/shard_map/psum | solution.py:104
  445.3 1.6 copy.73
  (89 shorter events, 14.1 us)
Async XLA Ops:
  7.2 94.5 %copy-start = (bf16[1024,32]{0,1:T(8,128)(2,1)S(1)}, bf16[1024,32]{0,1:T(8,128)(2,1)}, u32[]{:S(2)}) copy-start(bf16[1024,32]{0,1:T(8,128)(2,1)} %param.11) | copy-start | bytes 196612
  13.5 11.8 %copy-start.15 = (bf16[1,384,64]{1,2,0:T(8,128)(2,1)S(1)}, bf16[1,384,64]{1,2,0:T(8,128)(2,1)}, u32[]{:S(2)}) copy-start(bf16[1,384,64]{1,2,0:T(8,128)(2,1)} %param.14) | copy-start | bytes 147460
  14.7 38.2 %copy-start.16 = (bf16[1,64,384]{2,1,0:T(8,128)(2,1)S(1)}, bf16[1,64,384]{2,1,0:T(8,128)(2,1)}, u32[]{:S(2)}) copy-start(bf16[1,64,384]{2,1,0:T(8,128)(2,1)} %param.13) | copy-start | bytes 147460
  14.7 54.8 %copy-start.17 = (bf16[1,64,384]{2,1,0:T(8,128)(2,1)S(1)}, bf16[1,64,384]{2,1,0:T(8,128)(2,1)}, u32[]{:S(2)}) copy-start(bf16[1,64,384]{2,1,0:T(8,128)(2,1)} %param.12) | copy-start | bytes 147460
  14.7 72.7 %all-to-all-start = ((bf16[1,32,12,1024]{3,2,0,1:T(8,128)(2,1)}), bf16[1,32,12,1024]{3,2,0,1:T(8,128)(2,1)S(1)}, u32[]{:S(2)}, u32[]{:S(2)}) async-start(bf16[1,32,12,1024]{3,2,0,1:T(8,128)(2,1)} %bitcast.4), calls=%async_computation | async-start | bytes 2097152 | tf_op jit(solution)/shard_map/all_to_all | solution.py:21
  69.5 18.7 %copy-start.2 = (bf16[1,1024,384]{2,1,0:T(8,128)(2,1)}, bf16[1,1024,384]{2,1,0:T(8,128)(2,1)S(1)}, u32[]{:S(2)}) copy-start(bf16[1,1024,384]{2,1,0:T(8,128)(2,1)S(1)} %all-gather.1) | copy-start | bytes 2359300
  87.4 0.9 copy-start.4
  88.3 0.8 copy-start.12
  88.3 1.6 copy-start.6
  89.1 0.8 copy-start.10
  90.5 10.9 %copy-start.18 = (s32[128,2]{0,1:T(2,128)S(1)}, s32[128,2]{0,1:T(2,128)}, u32[]{:S(2)}) copy-start(s32[128,2]{0,1:T(2,128)} %param.10) | copy-start | bytes 3076
  91.8 9.9 %copy-start.7 = (bf16[128,1024]{1,0:T(8,128)(2,1)S(1)}, bf16[128,1024]{1,0:T(8,128)(2,1)}, u32[]{:S(2)}) copy-start(bf16[128,1024]{1,0:T(8,128)(2,1)} %param.9) | copy-start | bytes 786436
  91.8 36.3 %all-to-all-start.1 = ((bf16[1,32,12,1024]{3,2,0,1:T(8,128)(2,1)}), bf16[1,32,12,1024]{3,2,0,1:T(8,128)(2,1)S(1)}, u32[]{:S(2)}, u32[]{:S(2)}) async-start(bf16[1,32,12,1024]{3,2,0,1:T(8,128)(2,1)} %bitcast.8), calls=%async_computation.1 | async-start | bytes 2097152 | tf_op jit(solution)/shard_map/all_to_all | solution.py:21
  101.9 2.2 copy-start.14
  129.8 1.2 copy-start.8
  129.8 1.5 copy-start.1
  167.1 2.0 copy-start.5
  167.3 1.8 copy-start.11
  167.3 1.8 copy-start.13
  169.1 1.1 copy-start.3
  172.1 6.9 %copy-start.9 = (bf16[128,2,1024]{2,1,0:T(2,128)(2,1)S(1)}, bf16[128,2,1024]{2,1,0:T(2,128)(2,1)}, u32[]{:S(2)}) copy-start(bf16[128,2,1024]{2,1,0:T(2,128)(2,1)} %copy-done.8) | copy-start | bytes 1572868
  172.1 32.0 %all-to-all-start.3 = ((bf16[1,32,12,1024]{3,2,0,1:T(8,128)(2,1)}), bf16[1,32,12,1024]{3,2,0,1:T(8,128)(2,1)S(1)}, u32[]{:S(2)}, u32[]{:S(2)}) async-start(bf16[1,32,12,1024]{3,2,0,1:T(8,128)(2,1)} %bitcast.10), calls=%async_computation.3 | async-start | bytes 2097152 | tf_op jit(solution)/shard_map/all_to_all | solution.py:21
  178.1 267.3 %all-reduce.3.cloned.1.call-start = ((), (), s32[]{:S(2)}) async-start(), calls=%async_computation.4 | async-start | bytes 262144 | tf_op jit(solution)/shard_map/psum | solution.py:104
Sparse Core Ops, SparseCore 0:
  184.5 260.8 all-reduce.2
where the time goes:
time: 454 us
  waiting for transfers between devices  282 us (62%)
  blocking collectives  95.7 us (21%)
  starting transfers between devices  26.3 us (6%)
  local copies, waits for them, and re-layouts  20.4 us (4%)
  between operations  14.4 us (3%)
  matrix products  7.95 us (2%)
  other arithmetic  7.16 us (2%)
    psum x1, waiting for transfers between devices, on_device(): router_grad = lax.psum(router_part, ('dp', 'tp', 'cp'))  237 us
    all_to_all x3, waiting for transfers between devices, trade(): lax.all_to_all(shaped, ('tp', 'cp'), split_axis=1, concat_axis=1, tiled=T...  44.8 us
    all_to_all x1, blocking collectives, trade(): lax.all_to_all(shaped, ('tp', 'cp'), split_axis=1, concat_axis=1, tiled=T...  33.6 us
    all_gather x1, blocking collectives, on_device(): lax.all_gather(down_weight[0], 'dp', axis=1, tiled=True)  27.5 us
    all_to_all x3, starting transfers between devices, trade(): lax.all_to_all(shaped, ('tp', 'cp'), split_axis=1, concat_axis=1, tiled=T...  26.3 us
    all_gather x1, blocking collectives, on_device(): lax.all_gather(gate_weight[0], 'dp', axis=0, tiled=True)  17.9 us
    all_gather x1, blocking collectives, on_device(): lax.all_gather(up_weight[0], 'dp', axis=0, tiled=True)  16.6 us
  transfers between devices with their start and end apart: 4, of which 3 were waited for; matrix products, arithmetic and copies ran while one was open for 3% of the time, Pallas kernels for 0%

commit v1 on v0

--- a/solution.py
+++ b/solution.py
@@ -56,7 +56,9 @@
     contract = (((1,), (1,)), ((), ()))
     w_gate, w_up, w_down = (
         lax.all_gather(gate_weight[0], "dp", axis=0, tiled=True),
-        lax.all_gather(up_weight[0], "dp", axis=0, tiled=True),
+        jnp.concatenate(
+            lax.all_to_all(jnp.stack([up_weight[0]] * lax.axis_size("dp")), "dp", 0, 0), axis=0
+        ),
         lax.all_gather(down_weight[0], "dp", axis=1, tiled=True),
     )
     logits = jnp.dot(tokens, router_weight, preferred_element_type=jnp.float32)

time: 454 us -> 481 us (1.059)
  blocking collectives: 95.7 us -> 123 us
    all_to_all x1 -> x2, blocking collectives: 33.6 us -> 70.6 us  [trade(): lax.all_to_all(shaped, ('tp', 'cp'), split_axis=1, concat_axis=1, tiled=T...]
    all_gather x1 -> x0, blocking collectives: 16.6 us -> none  [on_device(): lax.all_gather(up_weight[0], 'dp', axis=0, tiled=True)]
    all_to_all x3 -> x2, starting transfers between devices: 26.3 us -> 10.9 us  [trade(): lax.all_to_all(shaped, ('tp', 'cp'), split_axis=1, concat_axis=1, tiled=T...]
    all_to_all x0 -> x1, starting transfers between devices: none -> 13.1 us  [on_device(): lax.all_to_all(jnp.stack([up_weight[0]] * lax.axis_size('dp')), 'dp', 0, 0)]
    all_gather x1, blocking collectives: 27.5 us -> 35.3 us  [on_device(): lax.all_gather(down_weight[0], 'dp', axis=1, tiled=True)]
    all_to_all x3 -> x2, waiting for transfers between devices: 44.8 us -> 44.8 us  [trade(): lax.all_to_all(shaped, ('tp', 'cp'), split_axis=1, concat_axis=1, tiled=T...]
where the time goes in v1:
time: 481 us
  waiting for transfers between devices  284 us (59%)
  blocking collectives  123 us (26%)
  starting transfers between devices  24 us (5%)
  local copies, waits for them, and re-layouts  20.4 us (4%)
  between operations  14.5 us (3%)
  matrix products  7.96 us (2%)
  other arithmetic  7.34 us (2%)
    psum x1, waiting for transfers between devices, on_device(): router_grad = lax.psum(router_part, ('dp', 'tp', 'cp'))  239 us
    all_to_all x2, blocking collectives, trade(): lax.all_to_all(shaped, ('tp', 'cp'), split_axis=1, concat_axis=1, tiled=T...  70.6 us
    all_to_all x2, waiting for transfers between devices, trade(): lax.all_to_all(shaped, ('tp', 'cp'), split_axis=1, concat_axis=1, tiled=T...  44.8 us
    all_gather x1, blocking collectives, on_device(): lax.all_gather(down_weight[0], 'dp', axis=1, tiled=True)  35.3 us
    all_gather x1, blocking collectives, on_device(): lax.all_gather(gate_weight[0], 'dp', axis=0, tiled=True)  16.7 us
    all_to_all x1, starting transfers between devices, on_device(): lax.all_to_all(jnp.stack([up_weight[0]] * lax.axis_size('dp')), 'dp', 0, 0)  13.1 us
    all_to_all x2, starting transfers between devices, trade(): lax.all_to_all(shaped, ('tp', 'cp'), split_axis=1, concat_axis=1, tiled=T...  10.9 us
  transfers between devices with their start and end apart: 4, of which 3 were waited for; matrix products, arithmetic and copies ran while one was open for 3% of the time, Pallas kernels for 0%

profile of v1, /device:TPU:1, one launch (start us, length us, event | category | flops | bytes accessed | tf_op | source)
XLA Modules:
  0.0 480.5 jit_solution(9443765154305707901)
XLA Ops:
  10.1 1.2 broadcast_in_dim.16
  11.6 1.9 scatter_custom_fusion
  13.7 37.2 %all_to_all.25 = bf16[1,32,12,1024]{3,2,0,1:T(8,128)(2,1)S(1)} all-to-all(bf16[1,32,12,1024]{3,2,0,1:T(8,128)(2,1)S(1)} %bitcast.71), channel_id=1, replica_groups=mesh['dp'=16,'tp'=4,'cp'=8] {'tp','cp'}, dimensions={1} | all-to-all | bytes 1572864 | tf_op jit(solution)/shard_map/all_to_all | solution.py:21
  51.9 13.1 %all-to-all-start.1 = ((bf16[16,64,384]{2,1,0:T(8,128)(2,1)}), bf16[16,64,384]{2,1,0:T(8,128)(2,1)S(1)}, u32[]{:S(2)}, u32[]{:S(2)}) async-start(bf16[16,64,384]{2,1,0:T(8,128)(2,1)} %stack.3), calls=%async_computation.1 | async-start | bytes 1572864 | tf_op jit(solution)/shard_map/all_to_all | solution.py:60
  65.0 35.3 %all-gather.1 = bf16[1,384,1024]{1,2,0:T(8,128)(2,1)} all-gather(bf16[1,384,64]{1,2,0:T(8,128)(2,1)S(1)} %copy-done.16), channel_id=3, replica_groups=mesh['dp'=16,'tp'=4,'cp'=8] {'dp'}, dimensions={2}, use_global_device_ids=true | all-gather | bytes 835584 | tf_op jit(solution)/shard_map/all_gather | solution.py:62
  100.3 16.7 %all-gather = bf16[1,1024,384]{2,1,0:T(8,128)(2,1)S(1)} all-gather(bf16[1,64,384]{2,1,0:T(8,128)(2,1)S(1)} %copy-done.17), channel_id=2, replica_groups=mesh['dp'=16,'tp'=4,'cp'=8] {'dp'}, dimensions={1}, use_global_device_ids=true | all-gather | bytes 835584 | tf_op jit(solution)/shard_map/all_gather | solution.py:58
  120.1 1.2 reshape_broadcast_in_dim.6
  121.3 4.8 %all-to-all-start.2 = ((bf16[1,32,12,1024]{3,2,0,1:T(8,128)(2,1)}), bf16[1,32,12,1024]{3,2,0,1:T(8,128)(2,1)S(1)}, u32[]{:S(2)}, u32[]{:S(2)}) async-start(bf16[1,32,12,1024]{3,2,0,1:T(8,128)(2,1)} %bitcast.9), calls=%async_computation.2 | async-start | bytes 2097152 | tf_op jit(solution)/shard_map/all_to_all | solution.py:21
  126.6 2.0 gather_fusion
  129.1 1.7 mul.98
  130.9 21.9 %all-to-all-done.2 = bf16[1,32,12,1024]{3,2,0,1:T(8,128)(2,1)S(1)} async-done(((bf16[1,32,12,1024]{3,2,0,1:T(8,128)(2,1)}), bf16[1,32,12,1024]{3,2,0,1:T(8,128)(2,1)S(1)}, u32[]{:S(2)}, u32[]{:S(2)}) %all-to-all-start.2) | async-done | bytes 786464 | tf_op jit(solution)/shard_map/all_to_all | solution.py:21
  153.0 1.2 gather_fusion.1
  154.6 1.1 fusion.10
  156.1 2.2 scatter_custom_fusion.1
  158.4 33.4 %all_to_all.26 = bf16[1,32,12,1024]{3,2,0,1:T(8,128)(2,1)S(1)} all-to-all(bf16[1,32,12,1024]{3,2,0,1:T(8,128)(2,1)S(1)} %bitcast.72), channel_id=1, replica_groups=mesh['dp'=16,'tp'=4,'cp'=8] {'tp','cp'}, dimensions={1} | all-to-all | bytes 1572864 | tf_op jit(solution)/shard_map/all_to_all | solution.py:21
  192.1 1.8 fusion.1
  195.7 1.2 reshape_broadcast_in_dim.7
  196.8 6.0 %all-to-all-start.4 = ((bf16[1,32,12,1024]{3,2,0,1:T(8,128)(2,1)}), bf16[1,32,12,1024]{3,2,0,1:T(8,128)(2,1)S(1)}, u32[]{:S(2)}, u32[]{:S(2)}) async-start(bf16[1,32,12,1024]{3,2,0,1:T(8,128)(2,1)} %bitcast.11), calls=%async_computation.4 | async-start | bytes 2097152 | tf_op jit(solution)/shard_map/all_to_all | solution.py:21
  203.8 2.1 multiply_reduce_fusion
  205.9 22.9 %all-to-all-done.4 = bf16[1,32,12,1024]{3,2,0,1:T(8,128)(2,1)S(1)} async-done(((bf16[1,32,12,1024]{3,2,0,1:T(8,128)(2,1)}), bf16[1,32,12,1024]{3,2,0,1:T(8,128)(2,1)S(1)}, u32[]{:S(2)}, u32[]{:S(2)}) %all-to-all-start.4) | async-done | bytes 786464 | tf_op jit(solution)/shard_map/all_to_all | solution.py:21
  229.0 1.2 gather_fusion.2
  230.9 1.2 reduce_sum.60
  233.1 239.0 %all-reduce.3.cloned.1.call-done = f32[1024,32]{0,1:T(8,128)} async-done(((f32[1024,32]{0,1:T(8,128)}), f32[1024,32]{0,1:T(8,128)}) %all-reduce.3.cloned.1.call-update) | async-done | bytes 131088 | tf_op jit(solution)/shard_map/psum | solution.py:106
  472.1 1.6 copy.73
  (90 shorter events, 14.1 us)
Async XLA Ops:
  7.2 119.3 %copy-start = (bf16[1024,32]{0,1:T(8,128)(2,1)S(1)}, bf16[1024,32]{0,1:T(8,128)(2,1)}, u32[]{:S(2)}) copy-start(bf16[1024,32]{0,1:T(8,128)(2,1)} %param.11) | copy-start | bytes 196612
  13.5 37.4 %copy-start.15 = (bf16[1,64,384]{2,1,0:T(8,128)(2,1)S(1)}, bf16[1,64,384]{2,1,0:T(8,128)(2,1)}, u32[]{:S(2)}) copy-start(bf16[1,64,384]{2,1,0:T(8,128)(2,1)} %param.13) | copy-start | bytes 147460
  50.9 14.1 %copy-start.16 = (bf16[1,384,64]{1,2,0:T(8,128)(2,1)S(1)}, bf16[1,384,64]{1,2,0:T(8,128)(2,1)}, u32[]{:S(2)}) copy-start(bf16[1,384,64]{1,2,0:T(8,128)(2,1)} %param.14) | copy-start | bytes 147460
  50.9 49.4 %copy-start.17 = (bf16[1,64,384]{2,1,0:T(8,128)(2,1)S(1)}, bf16[1,64,384]{2,1,0:T(8,128)(2,1)}, u32[]{:S(2)}) copy-start(bf16[1,64,384]{2,1,0:T(8,128)(2,1)} %param.12) | copy-start | bytes 147460
  51.9 65.3 %all-to-all-start.1 = ((bf16[16,64,384]{2,1,0:T(8,128)(2,1)}), bf16[16,64,384]{2,1,0:T(8,128)(2,1)S(1)}, u32[]{:S(2)}, u32[]{:S(2)}) async-start(bf16[16,64,384]{2,1,0:T(8,128)(2,1)} %stack.3), calls=%async_computation.1 | async-start | bytes 1572864 | tf_op jit(solution)/shard_map/all_to_all | solution.py:60
  116.9 0.9 copy-start.4
  117.1 1.3 copy-start.2
  117.8 0.8 copy-start.12
  117.8 1.6 copy-start.6
  118.6 0.8 copy-start.10
  120.1 6.1 %copy-start.18 = (s32[128,2]{0,1:T(2,128)S(1)}, s32[128,2]{0,1:T(2,128)}, u32[]{:S(2)}) copy-start(s32[128,2]{0,1:T(2,128)} %param.10) | copy-start | bytes 3076
  121.3 5.1 %copy-start.7 = (bf16[128,1024]{1,0:T(8,128)(2,1)S(1)}, bf16[128,1024]{1,0:T(8,128)(2,1)}, u32[]{:S(2)}) copy-start(bf16[128,1024]{1,0:T(8,128)(2,1)} %param.9) | copy-start | bytes 786436
  121.3 31.6 %all-to-all-start.2 = ((bf16[1,32,12,1024]{3,2,0,1:T(8,128)(2,1)}), bf16[1,32,12,1024]{3,2,0,1:T(8,128)(2,1)S(1)}, u32[]{:S(2)}, u32[]{:S(2)}) async-start(bf16[1,32,12,1024]{3,2,0,1:T(8,128)(2,1)} %bitcast.9), calls=%async_computation.2 | async-start | bytes 2097152 | tf_op jit(solution)/shard_map/all_to_all | solution.py:21
  126.6 2.2 copy-start.14
  154.5 1.2 copy-start.8
  154.5 1.5 copy-start.1
  191.9 2.0 copy-start.5
  192.0 1.8 copy-start.11
  192.1 1.8 copy-start.13
  193.9 1.1 copy-start.3
  196.8 6.9 %copy-start.9 = (bf16[128,2,1024]{2,1,0:T(2,128)(2,1)S(1)}, bf16[128,2,1024]{2,1,0:T(2,128)(2,1)}, u32[]{:S(2)}) copy-start(bf16[128,2,1024]{2,1,0:T(2,128)(2,1)} %copy-done.8) | copy-start | bytes 1572868
  196.8 31.9 %all-to-all-start.4 = ((bf16[1,32,12,1024]{3,2,0,1:T(8,128)(2,1)}), bf16[1,32,12,1024]{3,2,0,1:T(8,128)(2,1)S(1)}, u32[]{:S(2)}, u32[]{:S(2)}) async-start(bf16[1,32,12,1024]{3,2,0,1:T(8,128)(2,1)} %bitcast.11), calls=%async_computation.4 | async-start | bytes 2097152 | tf_op jit(solution)/shard_map/all_to_all | solution.py:21
  202.8 269.3 %all-reduce.3.cloned.1.call-start = ((), (), s32[]{:S(2)}) async-start(), calls=%async_computation.5 | async-start | bytes 262144 | tf_op jit(solution)/shard_map/psum | solution.py:106
Sparse Core Ops, SparseCore 0:
  209.2 262.8 all-reduce.2
